TPU v7x, 256 devices: a whole 4x4x8 slice. The times are simulated.
256 devices in a mesh: reg: 128 (over z, x, y), bat: 2 (over core).
Axes of the slice: x: 4, y: 4, z: 8, core: 2. Of those that a mesh axis runs over, the one named last changes fastest.
Arguments:
- top_flow: float32 [256, 32768], P('reg', 'bat'), may hold values from 0.25 to 4
- mid_logprob: float32 [384, 32768], P('reg', 'bat'), may hold values from -420 to -30
- low_logprob: float32 [512, 32768], P('reg', 'bat'), may hold values from -420 to -30
- top_weight: bfloat16 [256, 64, 4096], P('reg'), may hold values from 0.049804688 to 1
- mid_weight: bfloat16 [384, 64, 4096], P('reg'), may hold values from 0.049804688 to 1
- top_children: int32 [256, 2], replicated, may hold values from 0 to 383, all different within a row
- mid_children: int32 [384, 2], replicated, may hold values from 0 to 511, all different within a row
Outputs:
- low_flow: float32 [512, 32768], P('reg', 'bat')
- top_params: float32 [256, 64, 4096], P('reg', 'bat')
- mid_params: float32 [384, 64, 4096], P('reg', 'bat')
Inputs may be any that keep to these rules, and one draw needn't show every extreme that they name: `top_children`: each row names two different middle regions, and every middle region is named by some row. `mid_children`: each row names two different lower regions, and every lower region is named by some row.
All inputs are finite; a program needn't handle non-finite values.
Results may differ from a plain program's by a relative error of at most 0.0024.
Values may be sent and summed in bfloat16 or wider, within the bound.
A program may use at most 64 MiB of HBM per device.

v0:
```python
import jax
import jax.numpy as jnp
from jax import lax
from jax.sharding import PartitionSpec as P


def exponent(tables):
    return jnp.exp(tables - jnp.max(tables, axis=-1, keepdims=True)).astype(jnp.bfloat16)


def outer_of(left_vals, right_vals):
    row_count = left_vals.shape[0]
    components = left_vals.shape[1]
    product = left_vals.astype(jnp.float32)[:, :, None] * right_vals.astype(jnp.float32)[:, None, :]
    return product.reshape(row_count, components * components).astype(jnp.bfloat16)


def batch_values(logprob, components):
    reg_count = lax.axis_size("reg")
    local_count = logprob.shape[0]
    slice_width = logprob.shape[1] // reg_count
    arrived = lax.all_to_all(
        logprob.reshape(local_count, reg_count, slice_width),
        "reg",
        split_axis=1,
        concat_axis=0,
        tiled=True,
    )
    return exponent(arrived.reshape(local_count * reg_count, slice_width // components, components))


def region_pass(weight, flows, left_vals, right_vals):
    row_count = left_vals.shape[0]
    components = left_vals.shape[1]
    left_full = left_vals.astype(jnp.float32)
    right_full = right_vals.astype(jnp.float32)
    outers = outer_of(left_vals, right_vals)
    masses = lax.dot_general(
        outers, weight, (((1,), (1,)), ((), ())), preferred_element_type=jnp.float32
    )
    ratios = (flows / masses).astype(jnp.bfloat16)
    spread = jnp.dot(ratios, weight, preferred_element_type=jnp.float32).reshape(
        row_count, components, components
    )
    left_flow = left_full * jnp.einsum("xij,xj->xi", spread, right_full)
    right_flow = right_full * jnp.einsum("xij,xi->xj", spread, left_full)
    extra = lax.dot_general(
        ratios, outers, (((0,), (0,)), ((), ())), preferred_element_type=jnp.float32
    )
    return (left_flow, right_flow, extra)


def parameter_flows(weights, extra):
    bat_index = lax.axis_index("bat")
    half_width = weights.shape[1] // lax.axis_size("bat")
    weight_half = lax.dynamic_slice_in_dim(weights, bat_index * half_width, half_width, 1).astype(
        jnp.float32
    )
    summed = lax.psum_scatter(extra, "bat", scatter_dimension=1, tiled=True)
    return summed * weight_half


def layer(weights, flows, values, children):
    reg_count = lax.axis_size("reg")
    local_count = weights.shape[0]
    components = weights.shape[1]
    row_count = flows.shape[1] // components
    row_slice = values.shape[1]
    width = row_slice * components
    chosen = jnp.take(values, children, axis=0)
    owned = lax.all_to_all(
        chosen.reshape(reg_count, local_count, 2, 1, width),
        "reg",
        split_axis=0,
        concat_axis=3,
        tiled=True,
    )
    owned = owned.reshape(local_count, 2, row_count, components)
    left_flow, right_flow, extra = lax.map(
        lambda region_item: region_pass(
            region_item[0], region_item[1], region_item[2], region_item[3]
        ),
        (weights, flows.reshape(local_count, row_count, components), owned[:, 0], owned[:, 1]),
    )
    params = parameter_flows(weights, extra)
    both_sides = jnp.concatenate([left_flow, right_flow], axis=0)
    sliced = lax.all_to_all(
        both_sides.reshape(2 * local_count, reg_count, width),
        "reg",
        split_axis=1,
        concat_axis=0,
        tiled=True,
    )
    ids = jnp.transpose(children.reshape(reg_count, local_count, 2), (0, 2, 1)).reshape(-1)
    totals = jax.ops.segment_sum(sliced.reshape(-1, width), ids, num_segments=values.shape[0])
    child_count = values.shape[0] // reg_count
    returned = lax.all_to_all(
        totals.reshape(reg_count, child_count, 1, width),
        "reg",
        split_axis=0,
        concat_axis=2,
        tiled=True,
    )
    return (returned.reshape(child_count, row_count * components), params)


def shards(top_flow, mid_logprob, low_logprob, top_weight, mid_weight, top_children, mid_children):
    components = top_weight.shape[1]
    mid_values = batch_values(mid_logprob, components)
    low_values = batch_values(low_logprob, components)
    mid_flow, top_params = layer(top_weight, top_flow, mid_values, top_children)
    low_flow, mid_params = layer(mid_weight, mid_flow, low_values, mid_children)
    return (low_flow, top_params, mid_params)


def solution(mesh):
    return jax.shard_map(
        shards,
        mesh=mesh,
        in_specs=(
            P("reg", "bat"),
            P("reg", "bat"),
            P("reg", "bat"),
            P("reg", None, None),
            P("reg", None, None),
            P(),
            P(),
        ),
        out_specs=(P("reg", "bat"), P("reg", "bat", None), P("reg", "bat", None)),
        check_vma=False,
    )
```

profile of v0, /device:TPU:2, one launch (start us, length us, event | category | flops | bytes accessed | tf_op | source)
XLA Modules:
  0.0 233.5 jit_solution(9753190749257685329)
XLA Ops:
  7.2 15.4 %all-to-all-start.2 = ((f32[3,128,128]{2,0,1:T(4,128)}), f32[3,128,128]{2,0,1:T(4,128)S(1)}, u32[]{:S(2)}, u32[]{:S(2)}) async-start(f32[3,128,128]{2,0,1:T(4,128)} %bitcast.227), calls=%async_computation.2 | async-start | bytes 524288 | tf_op jit(solution)/shard_map/all_to_all | solution.py:22
  25.3 1.5 copy.38
  27.8 9.4 %all-to-all-done.2 = f32[3,128,128]{2,0,1:T(4,128)S(1)} async-done(((f32[3,128,128]{2,0,1:T(4,128)}), f32[3,128,128]{2,0,1:T(4,128)S(1)}, u32[]{:S(2)}, u32[]{:S(2)}) %all-to-all-start.2) | async-done | bytes 196640 | tf_op jit(solution)/shard_map/all_to_all | solution.py:22
  37.3 6.7 %all-to-all-start = ((f32[4,128,128]{2,0,1:T(4,128)}), f32[4,128,128]{2,0,1:T(4,128)S(1)}, u32[]{:S(2)}, u32[]{:S(2)}) async-start(f32[4,128,128]{2,0,1:T(4,128)} %bitcast.228), calls=%async_computation | async-start | bytes 524288 | tf_op jit(solution)/shard_map/all_to_all | solution.py:22
  44.8 2.1 gather_fusion.1
  48.1 9.2 %all-to-all-done = f32[4,128,128]{2,0,1:T(4,128)S(1)} async-done(((f32[4,128,128]{2,0,1:T(4,128)}), f32[4,128,128]{2,0,1:T(4,128)S(1)}, u32[]{:S(2)}, u32[]{:S(2)}) %all-to-all-start) | async-done | bytes 262176 | tf_op jit(solution)/shard_map/all_to_all | solution.py:22
  57.3 6.7 %all-to-all-start.3 = ((bf16[128,2,2,1,128]{4,2,1,3,0:T(2,128)(2,1)}), bf16[128,2,2,1,128]{4,2,1,3,0:T(2,128)(2,1)S(1)}, u32[]{:S(2)}, u32[]{:S(2)}) async-start(bf16[128,2,2,1,128]{4,2,1,3,0:T(2,128)(2,1)} %fusion.19), calls=%async_computation.3 | async-start | bytes 262144 | tf_op jit(solution)/shard_map/all_to_all | solution.py:71
  65.0 10.9 %all-to-all-done.3 = bf16[128,2,2,1,128]{4,2,1,3,0:T(2,128)(2,1)S(1)} async-done(((bf16[128,2,2,1,128]{4,2,1,3,0:T(2,128)(2,1)}), bf16[128,2,2,1,128]{4,2,1,3,0:T(2,128)(2,1)S(1)}, u32[]{:S(2)}, u32[]{:S(2)}) %all-to-all-start.3) | async-done | bytes 131104 | tf_op jit(solution)/shard_map/all_to_all | solution.py:71
  76.3 12.0 %while.28 = (s32[]{:T(128)}, f32[2,256,64]{1,2,0:T(8,128)}, f32[2,256,64]{1,2,0:T(8,128)}, f32[2,64,4096]{2,1,0:T(8,128)}, bf16[2,256,64]{1,2,0:T(8,128)(2,1)S(1...) while((s32[]{:T(128)}, f32[2,256,64]{1,2,0:T(8,128)}, ...), condition=%wide.region_2.3_spmd, body=%wide.region_1.0_spmd.sunk | while | flops 409042944 | bytes 38831392 | solution.py:79
  90.5 6.7 %all-to-all-start.4 = ((f32[4,128,128]{2,0,1:T(4,128)}), f32[4,128,128]{2,0,1:T(4,128)S(1)}, u32[]{:S(2)}, u32[]{:S(2)}) async-start(f32[4,128,128]{2,0,1:T(4,128)} %copy.54), calls=%async_computation.4 | async-start | bytes 524288 | tf_op jit(solution)/shard_map/all_to_all | solution.py:87
  97.9 2.9 %gather_fusion = bf16[768,2,64]{2,1,0:T(2,128)(2,1)S(1)} fusion(bf16[512,2,64]{2,1,0:T(2,128)(2,1)S(1)} %fusion.15, s32[1024]{0:T(1024)S(1)} %pad_clamp_fusion.1), kind=kCustom, calls=%fused_computation | custom fusion | bytes 396288 | tf_op jit(solution)/shard_map/jit(_take)/gather | solution.py:70
  101.0 1.2 fusion.18
  102.3 8.3 %all-to-all-done.4 = f32[4,128,128]{2,0,1:T(4,128)S(1)} async-done(((f32[4,128,128]{2,0,1:T(4,128)}), f32[4,128,128]{2,0,1:T(4,128)S(1)}, u32[]{:S(2)}, u32[]{:S(2)}) %all-to-all-start.4) | async-done | bytes 262176 | tf_op jit(solution)/shard_map/all_to_all | solution.py:87
  110.6 6.7 %all-to-all-start.1 = ((bf16[128,3,2,1,128]{4,2,1,3,0:T(2,128)(2,1)}), bf16[128,3,2,1,128]{4,2,1,3,0:T(2,128)(2,1)S(1)}, u32[]{:S(2)}, u32[]{:S(2)}) async-start(bf16[128,3,2,1,128]{4,2,1,3,0:T(2,128)(2,1)} %fusion.18), calls=%async_computation.1 | async-start | bytes 393216 | tf_op jit(solution)/shard_map/all_to_all | solution.py:71
  117.7 2.9 %scatter_custom_fusion = f32[384,128]{1,0:T(8,128)} fusion(s32[512]{0:T(512)S(1)} %reshape.188, f32[512,128]{1,0:T(8,128)S(1)} %bitcast.229, f32[]{:T(128)} %constant.53.clone.1), kind=kCustom, calls=%fused_computation.56 | custom fusion | flops 65536 | bytes 196612 | tf_op jit(solution)/shard_map/scatter-add | solution.py:95
  120.6 9.3 %all-to-all-done.1 = bf16[128,3,2,1,128]{4,2,1,3,0:T(2,128)(2,1)S(1)} async-done(((bf16[128,3,2,1,128]{4,2,1,3,0:T(2,128)(2,1)}), bf16[128,3,2,1,128]{4,2,1,3,0:T(2,128)(2,1)S(1)}, u32[]{:S(2)}, u32[]{:S(2)}) %all-to-all-start.1) | async-done | bytes 196640 | tf_op jit(solution)/shard_map/all_to_all | solution.py:71
  129.9 6.6 %all-to-all-start.5 = ((f32[128,3,1,128]{3,2,1,0:T(1,128)}), f32[128,3,1,128]{3,2,1,0:T(1,128)S(1)}, u32[]{:S(2)}, u32[]{:S(2)}) async-start(f32[128,3,1,128]{3,2,1,0:T(1,128)} %bitcast.44), calls=%async_computation.5 | async-start | bytes 393216 | tf_op jit(solution)/shard_map/all_to_all | solution.py:97
  137.8 11.3 %all-to-all-done.5 = f32[128,3,1,128]{3,2,1,0:T(1,128)S(1)} async-done(((f32[128,3,1,128]{3,2,1,0:T(1,128)}), f32[128,3,1,128]{3,2,1,0:T(1,128)S(1)}, u32[]{:S(2)}, u32[]{:S(2)}) %all-to-all-start.5) | async-done | bytes 196640 | tf_op jit(solution)/shard_map/all_to_all | solution.py:97
  149.4 20.9 %while.29 = (s32[]{:T(128)}, f32[3,256,64]{1,2,0:T(8,128)S(1)}, f32[3,256,64]{1,2,0:T(8,128)S(1)}, f32[3,64,4096]{2,1,0:T(8,128)}, bf16[3,256,64]{1,2,0:T(8,128)...) while((s32[]{:T(128)}, f32[3,256,64]{1,2,0:T(8,128)S(1)}, ...), condition=%wide.region_6.7_spmd, body=%wide.region_5.6_spmd.sunk | while | flops 409042944 | bytes 19956856 | solution.py:79
  151.7 1.7 fusion.60
  153.4 1.7 fusion.61
  158.7 1.5 fusion.60
  160.3 1.8 fusion.61
  165.7 1.5 fusion.60
  167.2 1.7 fusion.61
  171.8 6.5 %all-to-all-start.6 = ((f32[6,128,128]{2,0,1:T(8,128)}), f32[6,128,128]{2,0,1:T(8,128)S(1)}, u32[]{:S(2)}, u32[]{:S(2)}) async-start(f32[6,128,128]{2,0,1:T(8,128)} %copy.62), calls=%async_computation.6 | async-start | bytes 1048576 | tf_op jit(solution)/shard_map/all_to_all | solution.py:87
  178.8 15.5 %all-to-all-done.6 = f32[6,128,128]{2,0,1:T(8,128)S(1)} async-done(((f32[6,128,128]{2,0,1:T(8,128)}), f32[6,128,128]{2,0,1:T(8,128)S(1)}, u32[]{:S(2)}, u32[]{:S(2)}) %all-to-all-start.6) | async-done | bytes 393248 | tf_op jit(solution)/shard_map/all_to_all | solution.py:87
  194.4 6.7 %scatter_custom_fusion.1 = f32[512,128]{1,0:T(8,128)} fusion(s32[768]{0:T(1024)S(1)} %reshape.196, f32[768,128]{1,0:T(8,128)S(1)} %reshape.198, f32[]{:T(128)} %constant.53.clone.1), kind=kCustom, calls=%fused_computation.54 | custom fusion | flops 98304 | bytes 262148 | tf_op jit(solution)/shard_map/scatter-add | solution.py:95
  201.1 6.6 %all-to-all-start.7 = ((f32[128,4,1,128]{3,1,2,0:T(4,128)}), f32[128,4,1,128]{3,1,2,0:T(4,128)S(1)}, u32[]{:S(2)}, u32[]{:S(2)}) async-start(f32[128,4,1,128]{3,1,2,0:T(4,128)} %bitcast.51), calls=%async_computation.7 | async-start | bytes 524288 | tf_op jit(solution)/shard_map/all_to_all | solution.py:97
  207.7 13.3 %all-to-all-done.7 = f32[128,4,1,128]{3,1,2,0:T(4,128)S(1)} async-done(((f32[128,4,1,128]{3,1,2,0:T(4,128)}), f32[128,4,1,128]{3,1,2,0:T(4,128)S(1)}, u32[]{:S(2)}, u32[]{:S(2)}) %all-to-all-start.7) | async-done | bytes 262176 | tf_op jit(solution)/shard_map/all_to_all | solution.py:97
  221.0 2.3 convert_multiply_fusion.1
  223.3 2.7 %convert_multiply_fusion = f32[3,32,4096]{2,1,0:T(8,128)} fusion(f32[3,32,4096]{2,1,0:T(8,128)} %reduce-scatter.5.cloned.1.call-done, bf16[3,64,4096]{2,1,0:T(8,128)(2,1)S(1)} %copy-done.1, s32[]{:T(128)S(6)} %select_n.40), kind=kLoop, calls=%fused_computation.36 | loop fusion | flops 786432 | bytes 3932164 | tf_op jit(solution)/shard_map/mul | solution.py:60
  (143 shorter events, 37.2 us)
Async XLA Ops:
  7.2 30.1 %all-to-all-start.2 = ((f32[3,128,128]{2,0,1:T(4,128)}), f32[3,128,128]{2,0,1:T(4,128)S(1)}, u32[]{:S(2)}, u32[]{:S(2)}) async-start(f32[3,128,128]{2,0,1:T(4,128)} %bitcast.227), calls=%async_computation.2 | async-start | bytes 524288 | tf_op jit(solution)/shard_map/all_to_all | solution.py:22
  37.2 26.7 %copy-start.10 = (s32[384,2]{0,1:T(2,128)S(1)}, s32[384,2]{0,1:T(2,128)}, u32[]{:S(2)}) copy-start(s32[384,2]{0,1:T(2,128)} %param.17) | copy-start | bytes 9220
  37.3 20.0 %all-to-all-start = ((f32[4,128,128]{2,0,1:T(4,128)}), f32[4,128,128]{2,0,1:T(4,128)S(1)}, u32[]{:S(2)}, u32[]{:S(2)}) async-start(f32[4,128,128]{2,0,1:T(4,128)} %bitcast.228), calls=%async_computation | async-start | bytes 524288 | tf_op jit(solution)/shard_map/all_to_all | solution.py:22
  44.0 20.3 %copy-start.5 = (f32[2,16384]{1,0:T(2,128)S(1)}, f32[2,16384]{1,0:T(2,128)}, u32[]{:S(2)}) copy-start(f32[2,16384]{1,0:T(2,128)} %param.11) | copy-start | bytes 393220
  47.1 29.2 %copy-start = (bf16[2,64,4096]{2,1,0:T(8,128)(2,1)S(1)}, bf16[2,64,4096]{2,1,0:T(8,128)(2,1)}, u32[]{:S(2)}) copy-start(bf16[2,64,4096]{2,1,0:T(8,128)(2,1)} %param.14) | copy-start | bytes 3145732
  57.3 18.6 %all-to-all-start.3 = ((bf16[128,2,2,1,128]{4,2,1,3,0:T(2,128)(2,1)}), bf16[128,2,2,1,128]{4,2,1,3,0:T(2,128)(2,1)S(1)}, u32[]{:S(2)}, u32[]{:S(2)}) async-start(bf16[128,2,2,1,128]{4,2,1,3,0:T(2,128)(2,1)} %fusion.19), calls=%async_computation.3 | async-start | bytes 262144 | tf_op jit(solution)/shard_map/all_to_all | solution.py:71
  76.9 1.6 copy-start.2
  79.3 1.4 copy-start.3
  80.6 0.9 copy-start.6
  80.6 1.0 copy-start.8
  81.6 0.7 copy-start.7
  81.6 0.7 copy-start.9
  82.9 1.6 copy-start.2
  85.3 1.4 copy-start.3
  86.6 0.9 copy-start.6
  86.6 1.0 copy-start.8
  87.6 0.7 copy-start.7
  87.6 0.7 copy-start.9
  90.5 10.5 %copy-start.4 = (pred[128,3,2]{2,1,0:T(4,128)(4,1)S(1)}, pred[128,3,2]{2,1,0:T(4,128)(4,1)}, u32[]{:S(2)}) copy-start(pred[128,3,2]{2,1,0:T(4,128)(4,1)} %copy.38) | copy-start | bytes 2308
  90.5 20.0 %all-to-all-start.4 = ((f32[4,128,128]{2,0,1:T(4,128)}), f32[4,128,128]{2,0,1:T(4,128)S(1)}, u32[]{:S(2)}, u32[]{:S(2)}) async-start(f32[4,128,128]{2,0,1:T(4,128)} %copy.54), calls=%async_computation.4 | async-start | bytes 524288 | tf_op jit(solution)/shard_map/all_to_all | solution.py:87
  97.3 20.0 %copy-start.11 = (s32[256,2]{0,1:T(2,128)S(1)}, s32[256,2]{0,1:T(2,128)}, u32[]{:S(2)}) copy-start(s32[256,2]{0,1:T(2,128)} %param.16) | copy-start | bytes 6148
  110.6 19.3 %all-to-all-start.1 = ((bf16[128,3,2,1,128]{4,2,1,3,0:T(2,128)(2,1)}), bf16[128,3,2,1,128]{4,2,1,3,0:T(2,128)(2,1)S(1)}, u32[]{:S(2)}, u32[]{:S(2)}) async-start(bf16[128,3,2,1,128]{4,2,1,3,0:T(2,128)(2,1)} %fusion.18), calls=%async_computation.1 | async-start | bytes 393216 | tf_op jit(solution)/shard_map/all_to_all | solution.py:71
  129.9 19.2 %all-to-all-start.5 = ((f32[128,3,1,128]{3,2,1,0:T(1,128)}), f32[128,3,1,128]{3,2,1,0:T(1,128)S(1)}, u32[]{:S(2)}, u32[]{:S(2)}) async-start(f32[128,3,1,128]{3,2,1,0:T(1,128)} %bitcast.44), calls=%async_computation.5 | async-start | bytes 393216 | tf_op jit(solution)/shard_map/all_to_all | solution.py:97
  136.4 84.5 %reduce-scatter.3.cloned.1.call-start = ((), (), s32[]{:S(2)}) async-start(), calls=%async_computation.10 | async-start | bytes 3145728 | tf_op jit(solution)/shard_map/reduce_scatter | solution.py:59
  137.2 86.1 %reduce-scatter.5.cloned.1.call-start = ((), (), s32[]{:S(2)}) async-start(), calls=%async_computation.11 | async-start | bytes 4718592 | tf_op jit(solution)/shard_map/reduce_scatter | solution.py:59
  171.8 22.5 %all-to-all-start.6 = ((f32[6,128,128]{2,0,1:T(8,128)}), f32[6,128,128]{2,0,1:T(8,128)S(1)}, u32[]{:S(2)}, u32[]{:S(2)}) async-start(f32[6,128,128]{2,0,1:T(8,128)} %copy.62), calls=%async_computation.6 | async-start | bytes 1048576 | tf_op jit(solution)/shard_map/all_to_all | solution.py:87
  194.3 28.9 %copy-start.1 = (bf16[3,64,4096]{2,1,0:T(8,128)(2,1)S(1)}, bf16[3,64,4096]{2,1,0:T(8,128)(2,1)}, u32[]{:S(2)}) copy-start(bf16[3,64,4096]{2,1,0:T(8,128)(2,1)} %get-tuple-element.366) | copy-start | bytes 4718596
  201.1 19.9 %all-to-all-start.7 = ((f32[128,4,1,128]{3,1,2,0:T(4,128)}), f32[128,4,1,128]{3,1,2,0:T(4,128)S(1)}, u32[]{:S(2)}, u32[]{:S(2)}) async-start(f32[128,4,1,128]{3,1,2,0:T(4,128)} %bitcast.51), calls=%async_computation.7 | async-start | bytes 524288 | tf_op jit(solution)/shard_map/all_to_all | solution.py:97
Sparse Core Ops, SparseCore 0:
  139.8 16.5 reduce-scatter.2
  170.4 9.7 reduce-scatter.4
where the time goes:
time: 235 us; the launch traced here: 234 us
  waiting for transfers between devices  87.9 us (37%)
  starting transfers between devices  62 us (26%)
  other arithmetic  27.6 us (12%)
  local copies, waits for them, and re-layouts  25.3 us (11%)
  matrix products  15.9 us (7%)
  between operations  14.5 us (6%)
    all_to_all x2, waiting for transfers between devices, layer(): lax.all_to_all(totals.reshape(reg_count, child_count, 1, width), 'reg', s...  24.6 us
    all_to_all x2, waiting for transfers between devices, layer(): lax.all_to_all(both_sides.reshape(2 * local_count, reg_count, width), 're...  23.8 us
    all_to_all x2, starting transfers between devices, batch_values(): lax.all_to_all(logprob.reshape(local_count, reg_count, slice_width), 'reg...  22.2 us
    all_to_all x2, waiting for transfers between devices, layer(): lax.all_to_all(chosen.reshape(reg_count, local_count, 2, 1, width), 'reg'...  20.2 us
    all_to_all x2, waiting for transfers between devices, batch_values(): lax.all_to_all(logprob.reshape(local_count, reg_count, slice_width), 'reg...  18.6 us
    all_to_all x2, starting transfers between devices, layer(): lax.all_to_all(chosen.reshape(reg_count, local_count, 2, 1, width), 'reg'...  13.4 us
    all_to_all x2, starting transfers between devices, layer(): lax.all_to_all(both_sides.reshape(2 * local_count, reg_count, width), 're...  13.2 us
    all_to_all x2, starting transfers between devices, layer(): lax.all_to_all(totals.reshape(reg_count, child_count, 1, width), 'reg', s...  13.2 us
  transfers between devices with their start and end apart: 10, of which 8 were waited for; matrix products, arithmetic and copies ran while one was open for 22% of the time, Pallas kernels for 0%

commit v1 on v0

v1 whole, which is shorter than its diff:
```python
import functools

import jax
import jax.numpy as jnp
from jax import lax
from jax.experimental import pallas as pl
from jax.experimental.pallas import tpu as pltpu
from jax.sharding import PartitionSpec as P

F32 = jnp.float32
BF16 = jnp.bfloat16
MESH = pl.DeviceIdType.MESH
LANES = 128


def exchange(peers, me, send_buf, recv_buf, send_sem, recv_sem):
    def one(step, carry):
        target = lax.rem(me + step, peers)
        pltpu.make_async_remote_copy(
            src_ref=send_buf.at[target],
            dst_ref=recv_buf.at[me],
            send_sem=send_sem,
            recv_sem=recv_sem,
            device_id={"reg": target},
            device_id_type=MESH,
        ).start()
        return carry

    lax.fori_loop(1, peers, one, 0)
    recv_buf[me] = send_buf[me]


def whole(peers, me, send_buf, recv_buf, send_sem, recv_sem):
    return pltpu.make_async_remote_copy(
        src_ref=send_buf.at[pl.ds(0, peers - 1)],
        dst_ref=recv_buf.at[pl.ds(0, peers - 1)],
        send_sem=send_sem,
        recv_sem=recv_sem,
        device_id={"reg": lax.rem(me + 1, peers)},
        device_id_type=MESH,
    )


def kernel(
    peers,
    comps,
    top_flow, mid_lp, low_lp, top_w, mid_w, top_ch, mid_ch,
    low_out, top_params, mid_params,
    flow_in, mid_in, low_in, tw, mw, tch, mch,
    stage, rows, edge_ids,
    pick_top, sum_top, pick_mid, sum_mid,
    w_turned, outers, lefts, rights, partials, mass_mid, flow_turned, ratios,
    moments, moments_in, params,
    s1m, r1m, s1l, r1l, s2t, r2t, s2m, r2m, s3, r3, s4, r4, s5, r5, s6, r6,
    in_sem, send_sem, recv_sem, mom_send, mom_recv, out_sem,
):
    me = lax.axis_index("reg")
    bat = lax.axis_index("bat")
    other = 1 - bat
    n_top = tw.shape[0]
    n_mid = mw.shape[0]
    n_low = low_in.shape[0]
    half = comps // 2
    pairs = flow_in.shape[1] // LANES
    wide = 2 * LANES

    loads = [
        pltpu.make_async_copy(src, dst, in_sem.at[slot])
        for slot, (src, dst) in enumerate(
            [(mid_lp, mid_in), (low_lp, low_in), (top_ch, tch), (mid_ch, mch),
             (top_flow, flow_in), (top_w, tw), (mid_w, mw)]
        )
    ]
    for load in loads:
        load.start()

    barrier = pltpu.get_barrier_semaphore()

    def greet(step, carry):
        pl.semaphore_signal(
            barrier, inc=1, device_id={"reg": lax.rem(me + step, peers)}, device_id_type=MESH
        )
        return carry

    lax.fori_loop(1, peers, greet, 0)
    pl.semaphore_signal(barrier, inc=1, device_id={"bat": other}, device_id_type=MESH)

    def chunk_rows(source, count):
        def some(group, carry):
            for u in range(8):
                c = group * 8 + u
                stage[pl.ds(pl.multiple_of(c * 8, 8), count), :] = source[
                    :, pl.ds(pl.multiple_of(c * LANES, LANES), LANES)
                ]
            return carry

        lax.fori_loop(0, pairs // 8, some, 0)

    def values_to_send(source, count, send_buf):
        chunk_rows(source, count)
        slots = send_buf.shape[1]
        for q in range(slots):
            if q >= count:
                rows[pl.ds(q, LANES, stride=slots), :] = jnp.zeros((LANES, LANES), F32)
                continue
            turned = stage[pl.ds(q, LANES, stride=8), :].T
            parts = []
            for par in range(2):
                part = turned[par * comps:(par + 1) * comps]
                parts.append(jnp.exp(part - jnp.max(part, axis=0, keepdims=True)))
            rows[pl.ds(q, LANES, stride=slots), :] = jnp.concatenate(parts, axis=0)
        send_buf[...] = rows[0:LANES * slots].astype(send_buf.dtype).reshape(send_buf.shape)

    def edge_table(children, grouped, slots):
        ids = children[...]
        if grouped != slots:
            ids = (ids // grouped) * slots + ids % grouped
        ids = ids.astype(F32)
        for t in range(children.shape[1] // LANES):
            for side in range(2):
                block = jnp.broadcast_to(
                    ids[side:side + 1, t * LANES:(t + 1) * LANES], (LANES, LANES)
                )
                edge_ids[pl.ds(2 * t * LANES + side, LANES, stride=2), :] = block.T

    def pick_table(edges, pick):
        ids = edge_ids[0:edges]
        lane = lax.broadcasted_iota(jnp.int32, (edges, LANES), 1).astype(F32)
        for t in range(pick.shape[1] // LANES):
            pick[:, t * LANES:(t + 1) * LANES] = jnp.where(
                ids == lane + float(t * LANES), 1.0, 0.0
            ).astype(BF16)

    def sum_table(edges, table):
        count = table.shape[0]
        row = lax.broadcasted_iota(jnp.int32, (count, LANES), 0).astype(F32)
        for t in range(edges // LANES):
            turned = edge_ids[t * LANES:(t + 1) * LANES].T
            table[:, t * LANES:(t + 1) * LANES] = jnp.where(
                row == turned[0:1], 1.0, 0.0
            ).astype(BF16)

    def matrix(recv_buf):
        return recv_buf[...].reshape(recv_buf.shape[0] * recv_buf.shape[1], LANES)

    def product(a, b):
        return lax.dot_general(a, b, (((1,), (0,)), ((), ())), preferred_element_type=F32)

    def unpack(recv_buf):
        slots = recv_buf.shape[1]
        rows[0:LANES * slots] = recv_buf[...].astype(F32).reshape(LANES * slots, LANES)

    def wide_row(q, slots):
        return jnp.concatenate(
            [rows[pl.ds(par * comps * slots + q, comps, stride=slots), :] for par in range(2)], axis=1
        )

    def put_wide(q, slots, value):
        for par in range(2):
            rows[pl.ds(par * comps * slots + q, comps, stride=slots), :] = value[
                :, par * LANES:(par + 1) * LANES
            ]

    def pack(send_buf):
        slots = send_buf.shape[1]
        send_buf[...] = rows[0:LANES * slots].astype(send_buf.dtype).reshape(send_buf.shape)

    def build_outer(slot):
        right = rights[slot].astype(BF16).reshape(comps // 16, 16, wide)

        def some(group, carry):
            for u in range(4):
                i = group * 4 + u
                left = jnp.broadcast_to(lefts[slot, pl.ds(i, 1), :], (16, wide)).astype(BF16)
                outers[slot, pl.ds(pl.multiple_of(i * comps, comps), comps), :] = (
                    right * left[None]
                ).reshape(comps, wide)
            return carry

        lax.fori_loop(0, comps // 4, some, 0)

    def flows_of(slot, ratio, q, slots):
        right = rights[slot]

        def block(b, right_acc):
            start = pl.multiple_of(b * 8 * comps, 8 * comps)
            spread = product(w_turned[slot, pl.ds(start, 8 * comps), :], ratio)
            for u in range(8):
                piece = spread[u * comps:(u + 1) * comps]
                left = lefts[slot, pl.ds(b * 8 + u, 1), :]
                right_acc = right_acc + piece * left
                folded = jnp.sum((piece * right).reshape(comps // 8, 8, wide), axis=0)
                at = pl.ds(pl.multiple_of((b * 8 + u) * 8, 8), 8)
                for par in range(2):
                    partials[par, at, :] = folded[:, par * LANES:(par + 1) * LANES]
            return right_acc

        right_acc = lax.fori_loop(0, comps // 8, block, jnp.zeros((comps, wide), F32))
        left_acc = jnp.concatenate(
            [
                functools.reduce(
                    lambda a, b: a + b,
                    [partials[par, pl.ds(sub, comps, stride=8), :] for sub in range(8)],
                )
                for par in range(2)
            ],
            axis=1,
        )
        put_wide(q, slots, left_acc * lefts[slot])
        put_wide(q + 1, slots, right_acc * right)

    def moment_of(slot):
        moments[slot] = lax.dot_general(
            ratios[slot], outers[slot], (((1,), (1,)), ((), ())), preferred_element_type=F32
        )

    def moment_copy(slot):
        return pltpu.make_async_remote_copy(
            src_ref=moments.at[slot, pl.ds(pl.multiple_of(other * half, half), half), :],
            dst_ref=moments_in.at[slot],
            send_sem=mom_send.at[slot],
            recv_sem=mom_recv.at[slot],
            device_id={"bat": other},
            device_id_type=MESH,
        )

    def finish_params(slot, weight):
        moment_copy(slot).wait_recv()
        own = pl.ds(pl.multiple_of(bat * half, half), half)
        params[slot] = (moments[slot, own, :] + moments_in[slot]) * weight[own, :].astype(F32)

    def phase(index, send_buf, recv_buf):
        return (peers, me, send_buf, recv_buf, send_sem.at[index], recv_sem.at[index])

    phases = [
        phase(index, a, b)
        for index, (a, b) in enumerate(
            [(s1m, r1m), (s1l, r1l), (s2t, r2t), (s2m, r2m), (s3, r3), (s4, r4), (s5, r5), (s6, r6)]
        )
    ]

    loads[0].wait()
    values_to_send(mid_in, n_mid, s1m)
    loads[1].wait()
    values_to_send(low_in, n_low, s1l)
    pl.semaphore_wait(barrier, peers)
    exchange(*phases[0])
    exchange(*phases[1])

    loads[2].wait()
    edge_table(tch, n_mid, s1m.shape[1])
    pick_table(pick_top.shape[0], pick_top)

    whole(*phases[0]).wait_recv()
    s2t[...] = product(pick_top[...], matrix(r1m)).astype(BF16).reshape(s2t.shape)
    exchange(*phases[2])

    sum_table(pick_top.shape[0], sum_top)
    loads[3].wait()
    edge_table(mch, n_low, s1l.shape[1])
    pick_table(pick_mid.shape[0], pick_mid)
    whole(*phases[1]).wait_recv()
    s2m[...] = product(pick_mid[...], matrix(r1l)).astype(BF16).reshape(s2m.shape)
    exchange(*phases[3])

    loads[5].wait()
    for r in range(n_top):
        w_turned[r] = tw[r].T
    loads[4].wait()
    chunk_rows(flow_in, n_top)
    for r in range(n_top):
        turned = stage[pl.ds(r, LANES, stride=8), :].T
        flow_turned[r] = jnp.concatenate([turned[0:comps], turned[comps:2 * comps]], axis=1)

    whole(*phases[2]).wait_recv()
    unpack(r2t)
    for r in range(n_top):
        lefts[r] = wide_row(2 * r, 2 * n_top)
        rights[r] = wide_row(2 * r + 1, 2 * n_top)
    for r in range(n_top):
        build_outer(r)
        mass = product(tw[r], outers[r])
        ratio = (flow_turned[r] / mass).astype(BF16)
        ratios[r] = ratio
        flows_of(r, ratio, 2 * r, 2 * n_top)
    pack(s3)
    exchange(*phases[4])

    for r in range(n_top):
        moment_of(r)
        moment_copy(r).start()
    sum_table(pick_mid.shape[0], sum_mid)

    whole(*phases[4]).wait_recv()
    s4[...] = product(sum_top[...], matrix(r3)).reshape(s4.shape)
    exchange(*phases[5])

    loads[6].wait()
    whole(*phases[3]).wait_recv()
    unpack(r2m)
    for r in range(n_mid):
        lefts[n_top + r] = wide_row(2 * r, 2 * n_mid)
        rights[n_top + r] = wide_row(2 * r + 1, 2 * n_mid)
    for r in range(n_mid):
        w_turned[n_top + r] = mw[r].T
        build_outer(n_top + r)
        mass_mid[r] = product(mw[r], outers[n_top + r])

    whole(*phases[5]).wait_recv()
    unpack(r4)
    for r in range(n_mid):
        flow_turned[r] = wide_row(r, r4.shape[1])
    for r in range(n_mid):
        ratio = (flow_turned[r] / mass_mid[r]).astype(BF16)
        ratios[n_top + r] = ratio
        flows_of(n_top + r, ratio, 2 * r, 2 * n_mid)
    pack(s5)
    exchange(*phases[6])

    outs = []
    for r in range(n_top):
        finish_params(r, tw.at[r])
        outs.append(pltpu.make_async_copy(params.at[r], top_params.at[r], out_sem.at[r]))
        outs[-1].start()
    for r in range(n_mid):
        moment_of(n_top + r)
        moment_copy(n_top + r).start()

    whole(*phases[6]).wait_recv()
    s6[...] = product(sum_mid[...], matrix(r5)).reshape(s6.shape)
    exchange(*phases[7])

    for r in range(n_mid):
        slot = n_top + r
        finish_params(slot, mw.at[r])
        outs.append(pltpu.make_async_copy(params.at[slot], mid_params.at[r], out_sem.at[slot]))
        outs[-1].start()

    whole(*phases[7]).wait_recv()
    unpack(r6)
    for q in range(n_low):
        low_out[q] = rows[pl.ds(q, LANES, stride=n_low), :].T

    for one in phases:
        whole(*one).wait_send()
    for slot in range(n_top + n_mid):
        moment_copy(slot).wait_send()
    for out in outs:
        out.wait()


def shards(top_flow, mid_logprob, low_logprob, top_weight, mid_weight, top_children, mid_children):
    peers = lax.axis_size("reg")
    n_top, comps, square = top_weight.shape
    n_mid = mid_weight.shape[0]
    n_low = low_logprob.shape[0]
    n_all = n_top + n_mid
    half = comps // 2
    wide = 2 * LANES
    mid_slots = 4
    top_edges = 2 * n_top
    mid_edges = 2 * n_mid
    vmem = pltpu.VMEM

    def pair(slots, kind=BF16):
        return [vmem((peers, slots, LANES), kind)] * 2

    low, top_params, mid_params = pl.pallas_call(
        functools.partial(kernel, peers, comps),
        out_shape=(
            jax.ShapeDtypeStruct((n_low, LANES, LANES), F32),
            jax.ShapeDtypeStruct((n_top, half, square), F32),
            jax.ShapeDtypeStruct((n_mid, half, square), F32),
        ),
        in_specs=[pl.BlockSpec(memory_space=pltpu.HBM)] * 7,
        out_specs=(
            pl.BlockSpec(memory_space=pltpu.VMEM),
            pl.BlockSpec(memory_space=pl.ANY),
            pl.BlockSpec(memory_space=pl.ANY),
        ),
        scratch_shapes=[
            vmem(top_flow.shape, F32),
            vmem(mid_logprob.shape, F32),
            vmem(low_logprob.shape, F32),
            vmem(top_weight.shape, BF16),
            vmem(mid_weight.shape, BF16),
            vmem(top_children.shape[::-1], jnp.int32),
            vmem(mid_children.shape[::-1], jnp.int32),
            vmem((8 * LANES, LANES), F32),
            vmem((LANES * mid_edges, LANES), F32),
            vmem((peers * mid_edges, LANES), F32),
            vmem((peers * top_edges, peers * mid_slots), BF16),
            vmem((peers * mid_slots, peers * top_edges), BF16),
            vmem((peers * mid_edges, peers * n_low), BF16),
            vmem((peers * n_low, peers * mid_edges), BF16),
            vmem((n_all, square, comps), BF16),
            vmem((n_all, square, wide), BF16),
            vmem((n_all, comps, wide), F32),
            vmem((n_all, comps, wide), F32),
            vmem((2, 8 * comps, LANES), F32),
            vmem((n_mid, comps, wide), F32),
            vmem((n_mid, comps, wide), F32),
            vmem((n_all, comps, wide), BF16),
            vmem((n_all, comps, square), F32),
            vmem((n_all, half, square), F32),
            vmem((n_all, half, square), F32),
            *pair(mid_slots), *pair(n_low), *pair(top_edges), *pair(mid_edges),
            *pair(top_edges), *pair(mid_slots, F32), *pair(mid_edges), *pair(n_low, F32),
            pltpu.SemaphoreType.DMA((7,)),
            pltpu.SemaphoreType.DMA((8,)),
            pltpu.SemaphoreType.DMA((8,)),
            pltpu.SemaphoreType.DMA((n_all,)),
            pltpu.SemaphoreType.DMA((n_all,)),
            pltpu.SemaphoreType.DMA((n_all,)),
        ],
        compiler_params=pltpu.CompilerParams(
            collective_id=0, has_side_effects=True, vmem_limit_bytes=60 * 1024 * 1024
        ),
    )(top_flow, mid_logprob, low_logprob, top_weight, mid_weight, top_children.T, mid_children.T)
    return low.reshape(low_logprob.shape), top_params, mid_params


def solution(mesh):
    return jax.shard_map(
        shards,
        mesh=mesh,
        in_specs=(
            P("reg", "bat"),
            P("reg", "bat"),
            P("reg", "bat"),
            P("reg", None, None),
            P("reg", None, None),
            P(),
            P(),
        ),
        out_specs=(P("reg", "bat"), P("reg", "bat", None), P("reg", "bat", None)),
        check_vma=False,
    )
```

time: 235 us -> 89.9 us (0.38)
  waiting for transfers between devices: 87.9 us -> 0 us
  Pallas kernels: 0 us -> 83.7 us
  starting transfers between devices: 62 us -> 0 us
  other arithmetic: 27.6 us -> 0 us
  local copies, waits for them, and re-layouts: 25.3 us -> 5.36 us
  matrix products: 15.9 us -> 0 us
  between operations: 14.5 us -> 0.65 us
    all_to_all x8 -> x0, waiting for transfers between devices: 87.3 us -> none  [the longest x2 24.6 us: layer(): lax.all_to_all(totals.reshape(reg_count, child_count, 1, width), 'reg', s...]
    pallas_call x0 -> x1, Pallas kernels: none -> 83.7 us  [shards(): pl.pallas_call(functools.partial(kernel, peers, comps), out_shape=(jax.Sh...]
    all_to_all x8 -> x0, starting transfers between devices: 61.9 us -> none  [the longest x2 22.2 us: batch_values(): lax.all_to_all(logprob.reshape(local_count, reg_count, slice_width), 'reg...]
    dot_general x15 -> x0, matrix products: 15.9 us -> none  [the longest x5 6.72 us: region_pass(): lax.dot_general(ratios, outers, (((0,), (0,)), ((), ())), preferred_eleme...]
    scatter-add x2 -> x0, other arithmetic: 9.59 us -> none  [layer(): jax.ops.segment_sum(sliced.reshape(-1, width), ids, num_segments=values.s...]
    dynamic_slice x10 -> x0, local copies, waits for them, and re-layouts: 5.78 us -> none  [layer(): lax.map(lambda region_item: region_pass(region_item[0], region_item[1], r...]
    gather x4 -> x0, local copies, waits for them, and re-layouts: 5.35 us -> none  [layer(): chosen = jnp.take(values, children, axis=0)]
    mul x2 -> x0, other arithmetic: 4.98 us -> none  [parameter_flows(): return summed * weight_half]
  transfers between devices with their start and end apart: 10 -> 0, of which waited for: 8 -> 0; matrix products, arithmetic and copies ran while one was open for 22% -> 0% of each run, Pallas kernels for 0% -> 0%
where the time goes in v1:
time: 89.9 us; the launch traced here: 89.7 us
  Pallas kernels  83.7 us (93%)
  local copies, waits for them, and re-layouts  5.36 us (6%)
    pallas_call x1, Pallas kernels, shards(): pl.pallas_call(functools.partial(kernel, peers, comps), out_shape=(jax.Sh...  83.7 us
    unnamed x5, local copies, waits for them, and re-layouts  5.36 us

profile of v1, /device:TPU:2, one launch (start us, length us, event | category | flops | bytes accessed | tf_op | source)
XLA Modules:
  0.0 89.7 jit_solution(1506952830931341176)
XLA Ops:
  0.6 83.7 %shard_map.94 = (f32[4,128,128]{2,1,0:T(8,128)}, f32[2,32,4096]{2,1,0:T(8,128)}, f32[3,32,4096]{2,1,0:T(8,128)}) custom-call(f32[2,16384]{1,0:T(2,128)} %top_flow.1, f32[3,16384]{1,0:T(4,128)} %mid_lp.1, f32[4,16384]{1,0:T(4,128)} %low_lp.1, bf16[2,64,4096]{2,1,0:T(8,128)(2,1)} %top_w.1, bf16[3,64,4096]{2,1,0:T(8,128)(2,1)} %mid_w.1, s32[2,256]{1,0:T(2,128)} %bitcast.9, ...), custom_call_target="tpu_custom_call" | custom-call | tf_op jit(solution)/shard_map/pallas_call | solution.py:368
  84.3 0.0 copy-start
  84.3 1.9 %copy.12 = f32[1,4,128,128]{3,1,2,0:T(4,128)} copy(f32[1,4,128,128]{3,2,1,0:T(8,128)} %bitcast.7) | data formatting | bytes 524288
  86.3 2.3 %copy.15 = f32[2,32,4096]{2,1,0:T(8,128)} copy(f32[2,32,4096]{2,1,0:T(8,128)} %get-tuple-element.13) | data formatting | bytes 2097152
  88.5 0.0 copy-done
  88.5 1.1 %copy.16 = f32[3,32,4096]{2,1,0:T(8,128)} copy(f32[3,32,4096]{2,1,0:T(8,128)S(1)} %copy-done) | data formatting | bytes 3145728
Async XLA Ops:
  84.3 4.2 %copy-start = (f32[3,32,4096]{2,1,0:T(8,128)S(1)}, f32[3,32,4096]{2,1,0:T(8,128)}, u32[]{:S(2)}) copy-start(f32[3,32,4096]{2,1,0:T(8,128)} %get-tuple-element.14) | copy-start | bytes 4718596

commit v2 on v1

--- a/solution.py
+++ b/solution.py
@@ -13,9 +13,24 @@
 LANES = 128
 
 
+def each_peer(peers, me, visit):
+    def one(step):
+        ahead = me + step
+        visit(jnp.where(ahead >= peers, ahead - peers, ahead))
+
+    def some(group, carry):
+        for u in range(1, 9):
+            one(group * 8 + u)
+        return carry
+
+    groups = (peers - 1) // 8
+    lax.fori_loop(0, groups, some, 0)
+    for step in range(groups * 8 + 1, peers):
+        one(step)
+
+
 def exchange(peers, me, send_buf, recv_buf, send_sem, recv_sem):
-    def one(step, carry):
-        target = lax.rem(me + step, peers)
+    def one(target):
         pltpu.make_async_remote_copy(
             src_ref=send_buf.at[target],
             dst_ref=recv_buf.at[me],
@@ -24,9 +39,8 @@
             device_id={"reg": target},
             device_id_type=MESH,
         ).start()
-        return carry
-
-    lax.fori_loop(1, peers, one, 0)
+
+    each_peer(peers, me, one)
     recv_buf[me] = send_buf[me]
 
 
@@ -76,13 +90,10 @@
 
     barrier = pltpu.get_barrier_semaphore()
 
-    def greet(step, carry):
-        pl.semaphore_signal(
-            barrier, inc=1, device_id={"reg": lax.rem(me + step, peers)}, device_id_type=MESH
-        )
-        return carry
-
-    lax.fori_loop(1, peers, greet, 0)
+    def greet(target):
+        pl.semaphore_signal(barrier, inc=1, device_id={"reg": target}, device_id_type=MESH)
+
+    each_peer(peers, me, greet)
     pl.semaphore_signal(barrier, inc=1, device_id={"bat": other}, device_id_type=MESH)
 
     def chunk_rows(source, count):
@@ -339,7 +350,17 @@
     whole(*phases[7]).wait_recv()
     unpack(r6)
     for q in range(n_low):
-        low_out[q] = rows[pl.ds(q, LANES, stride=n_low), :].T
+        stage[pl.ds(q, LANES, stride=8), :] = rows[pl.ds(q, LANES, stride=n_low), :].T
+
+    def some_out(group, carry):
+        for u in range(8):
+            c = group * 8 + u
+            low_out[:, pl.ds(pl.multiple_of(c * LANES, LANES), LANES)] = stage[
+                pl.ds(pl.multiple_of(c * 8, 8), n_low), :
+            ]
+        return carry
+
+    lax.fori_loop(0, pairs // 8, some_out, 0)
 
     for one in phases:
         whole(*one).wait_send()
@@ -368,7 +389,7 @@
     low, top_params, mid_params = pl.pallas_call(
         functools.partial(kernel, peers, comps),
         out_shape=(
-            jax.ShapeDtypeStruct((n_low, LANES, LANES), F32),
+            jax.ShapeDtypeStruct(low_logprob.shape, F32),
             jax.ShapeDtypeStruct((n_top, half, square), F32),
             jax.ShapeDtypeStruct((n_mid, half, square), F32),
         ),
@@ -417,7 +438,7 @@
             collective_id=0, has_side_effects=True, vmem_limit_bytes=60 * 1024 * 1024
         ),
     )(top_flow, mid_logprob, low_logprob, top_weight, mid_weight, top_children.T, mid_children.T)
-    return low.reshape(low_logprob.shape), top_params, mid_params
+    return low, top_params, mid_params
 
 
 def solution(mesh):

time: 89.9 us -> 90.5 us (level)
  no operation moved by 1% of the time
where the time goes in v2:
time: 90.5 us; the launch traced here: 90.3 us
  Pallas kernels  84.5 us (93%)
  local copies, waits for them, and re-layouts  5.2 us (6%)
    pallas_call x1, Pallas kernels, shards(): pl.pallas_call(functools.partial(kernel, peers, comps), out_shape=(jax.Sh...  84.5 us
    unnamed x5, local copies, waits for them, and re-layouts  5.2 us

profile of v2, /device:TPU:2, one launch (start us, length us, event | category | flops | bytes accessed | tf_op | source)
XLA Modules:
  0.0 90.3 jit_solution(8138051829742318141)
XLA Ops:
  0.6 84.5 %shard_map.94 = (f32[4,16384]{1,0:T(4,128)}, f32[2,32,4096]{2,1,0:T(8,128)}, f32[3,32,4096]{2,1,0:T(8,128)}) custom-call(f32[2,16384]{1,0:T(2,128)} %top_flow.1, f32[3,16384]{1,0:T(4,128)} %mid_lp.1, f32[4,16384]{1,0:T(4,128)} %low_lp.1, bf16[2,64,4096]{2,1,0:T(8,128)(2,1)} %top_w.1, bf16[3,64,4096]{2,1,0:T(8,128)(2,1)} %mid_w.1, s32[2,256]{1,0:T(2,128)} %bitcast.3, ...), custom_call_target="tpu_custom_call" | custom-call | tf_op jit(solution)/shard_map/pallas_call | solution.py:389
  85.1 0.0 copy-start
  85.1 1.8 %copy.13 = f32[4,16384]{1,0:T(4,128)} copy(f32[4,16384]{1,0:T(4,128)} %get-tuple-element.6) | data formatting | bytes 524288
  86.9 2.3 %copy.14 = f32[2,32,4096]{2,1,0:T(8,128)} copy(f32[2,32,4096]{2,1,0:T(8,128)} %get-tuple-element.7) | data formatting | bytes 2097152
  89.2 0.0 copy-done
  89.2 1.1 %copy.15 = f32[3,32,4096]{2,1,0:T(8,128)} copy(f32[3,32,4096]{2,1,0:T(8,128)S(1)} %copy-done) | data formatting | bytes 3145728
Async XLA Ops:
  85.1 4.1 %copy-start = (f32[3,32,4096]{2,1,0:T(8,128)S(1)}, f32[3,32,4096]{2,1,0:T(8,128)}, u32[]{:S(2)}) copy-start(f32[3,32,4096]{2,1,0:T(8,128)} %get-tuple-element.8) | copy-start | bytes 4718596

commit v3 on v2

--- a/solution.py
+++ b/solution.py
@@ -252,10 +252,10 @@
 
     loads[0].wait()
     values_to_send(mid_in, n_mid, s1m)
+    pl.semaphore_wait(barrier, peers)
+    exchange(*phases[0])
     loads[1].wait()
     values_to_send(low_in, n_low, s1l)
-    pl.semaphore_wait(barrier, peers)
-    exchange(*phases[0])
     exchange(*phases[1])
 
     loads[2].wait()
@@ -267,13 +267,6 @@
     exchange(*phases[2])
 
     sum_table(pick_top.shape[0], sum_top)
-    loads[3].wait()
-    edge_table(mch, n_low, s1l.shape[1])
-    pick_table(pick_mid.shape[0], pick_mid)
-    whole(*phases[1]).wait_recv()
-    s2m[...] = product(pick_mid[...], matrix(r1l)).astype(BF16).reshape(s2m.shape)
-    exchange(*phases[3])
-
     loads[5].wait()
     for r in range(n_top):
         w_turned[r] = tw[r].T
@@ -297,6 +290,12 @@
     pack(s3)
     exchange(*phases[4])
 
+    loads[3].wait()
+    edge_table(mch, n_low, s1l.shape[1])
+    pick_table(pick_mid.shape[0], pick_mid)
+    whole(*phases[1]).wait_recv()
+    s2m[...] = product(pick_mid[...], matrix(r1l)).astype(BF16).reshape(s2m.shape)
+    exchange(*phases[3])
     for r in range(n_top):
         moment_of(r)
         moment_copy(r).start()

time: 90.5 us -> 86.5 us (0.956)
  Pallas kernels: 84.5 us -> 80.2 us
    pallas_call x1, Pallas kernels: 84.5 us -> 80.2 us  [shards(): pl.pallas_call(functools.partial(kernel, peers, comps), out_shape=(jax.Sh...]
where the time goes in v3:
time: 86.5 us; the launch traced here: 86.1 us
  Pallas kernels  80.2 us (93%)
  local copies, waits for them, and re-layouts  5.2 us (6%)
    pallas_call x1, Pallas kernels, shards(): pl.pallas_call(functools.partial(kernel, peers, comps), out_shape=(jax.Sh...  80.2 us
    unnamed x5, local copies, waits for them, and re-layouts  5.2 us

profile of v3, /device:TPU:2, one launch (start us, length us, event | category | flops | bytes accessed | tf_op | source)
XLA Modules:
  0.0 86.1 jit_solution(10268663269248607540)
XLA Ops:
  0.6 80.2 %shard_map.94 = (f32[4,16384]{1,0:T(4,128)}, f32[2,32,4096]{2,1,0:T(8,128)}, f32[3,32,4096]{2,1,0:T(8,128)}) custom-call(f32[2,16384]{1,0:T(2,128)} %top_flow.1, f32[3,16384]{1,0:T(4,128)} %mid_lp.1, f32[4,16384]{1,0:T(4,128)} %low_lp.1, bf16[2,64,4096]{2,1,0:T(8,128)(2,1)} %top_w.1, bf16[3,64,4096]{2,1,0:T(8,128)(2,1)} %mid_w.1, s32[2,256]{1,0:T(2,128)} %bitcast.3, ...), custom_call_target="tpu_custom_call" | custom-call | tf_op jit(solution)/shard_map/pallas_call | solution.py:388
  80.8 0.0 copy-start
  80.9 1.8 %copy.13 = f32[4,16384]{1,0:T(4,128)} copy(f32[4,16384]{1,0:T(4,128)} %get-tuple-element.6) | data formatting | bytes 524288
  82.6 2.3 %copy.14 = f32[2,32,4096]{2,1,0:T(8,128)} copy(f32[2,32,4096]{2,1,0:T(8,128)} %get-tuple-element.7) | data formatting | bytes 2097152
  84.9 0.0 copy-done
  84.9 1.1 %copy.15 = f32[3,32,4096]{2,1,0:T(8,128)} copy(f32[3,32,4096]{2,1,0:T(8,128)S(1)} %copy-done) | data formatting | bytes 3145728
Async XLA Ops:
  80.8 4.1 %copy-start = (f32[3,32,4096]{2,1,0:T(8,128)S(1)}, f32[3,32,4096]{2,1,0:T(8,128)}, u32[]{:S(2)}) copy-start(f32[3,32,4096]{2,1,0:T(8,128)} %get-tuple-element.8) | copy-start | bytes 4718596
